TPU v7x, 32 devices: a whole 2x2x4 slice. The times are simulated.
32 devices in a mesh: row: 8 (over z, y), col: 4 (over x, core).
Axes of the slice: x: 2, y: 2, z: 4, core: 2. Of those that a mesh axis runs over, the one named last changes fastest.
Arguments:
- tensor: bfloat16 [1024, 64, 512], P('row', None, 'col'), may hold values from -6 to 6
- loss_kind: int32 [1024, 64, 512], P('row', None, 'col'), may hold values from 0 to 1, as said below
- factor_one: float32 [1024, 512], P(('row', 'col')), may hold values from -2 to 2
- factor_two: float32 [512, 512], P(('col', 'row')), may hold values from -2 to 2
- factor_three: float32 [64, 512], replicated, may hold values from -2 to 2
- first_one: float32 [1024, 512], P(('row', 'col')), may hold values from -0.03 to 0.03
- second_one: float32 [1024, 512], P(('row', 'col')), may hold values from 0.0005 to 0.05
- first_two: float32 [512, 512], P(('col', 'row')), may hold values from -0.03 to 0.03
- second_two: float32 [512, 512], P(('col', 'row')), may hold values from 0.0005 to 0.05
- first_three: float32 [64, 512], replicated, may hold values from -0.03 to 0.03
- second_three: float32 [64, 512], replicated, may hold values from 0.0005 to 0.05
Outputs:
- new_one: float32 [1024, 512], P(('row', 'col'))
- new_two: float32 [512, 512], P(('col', 'row'))
- new_three: float32 [64, 512], replicated
Inputs may be any that keep to these rules, and one draw needn't show every extreme that they name: loss_kind takes one value on each block of 128 first-mode by 128 second-mode indices (with all 64 third-mode ones), aligned to multiples of 128 and 128, and is 1 on exactly half of these blocks.
All inputs are finite; a program needn't handle non-finite values.
Results may differ from a plain program's by a relative error of at most 0.003.
Values may be sent and summed in bfloat16 or wider, within the bound.
A program may use at most 128 MiB of HBM per device.

v0:
```python
import math
import jax
import jax.numpy as jnp
from jax import lax
from jax.sharding import PartitionSpec as P

ITERS = 2
STEP = 10
learn_rate = 0.05
beta_one = 0.8
beta_two = 0.95
adam_eps = 1e-08


def loss_slope(rebuilt, values, kinds):
    excess = rebuilt - values
    huber_part = jnp.clip(excess, -1.0, 1.0)
    target = jnp.where(values > 0, 1.0, 0.0).astype(rebuilt.dtype)
    logit_part = jax.nn.sigmoid(rebuilt) - target
    return jnp.where(kinds == 1, logit_part, huber_part)


def adam_step(param, first, second, grad, counter):
    first = beta_one * first + (1.0 - beta_one) * grad
    second = beta_two * second + (1.0 - beta_two) * grad * grad
    corr_one = 1.0 - beta_one**counter
    corr_two = 1.0 - beta_two**counter
    param = param - learn_rate * (first / corr_one) / (jnp.sqrt(second / corr_two) + adam_eps)
    return (param, first, second)


def tile_grads(tensor, loss_kind, half_one, half_two, half_three, scales):
    tile_rows, tile_depth, tile_cols = tensor.shape
    rank_width = half_one.shape[1]
    one_f = half_one.astype(jnp.float32)
    three_f = half_three.astype(jnp.float32)
    scaled_rows = (
        (one_f[:, None, :] * three_f[None, :, :])
        .astype(jnp.bfloat16)
        .reshape(tile_rows * tile_depth, rank_width)
    )
    rebuilt = lax.dot_general(
        scaled_rows, half_two, (((1,), (1,)), ((), ())), preferred_element_type=jnp.float32
    )
    values = tensor.reshape(tile_rows * tile_depth, tile_cols).astype(jnp.float32)
    deriv_bf = loss_slope(
        rebuilt, values, loss_kind.reshape(tile_rows * tile_depth, tile_cols)
    ).astype(jnp.bfloat16)
    projected = jnp.dot(deriv_bf, half_two, preferred_element_type=jnp.float32).reshape(
        tile_rows, tile_depth, rank_width
    )
    grad_one = jnp.sum(projected * three_f[None, :, :], axis=1) * scales[0]
    grad_three = jnp.sum(projected * one_f[:, None, :], axis=0) * scales[2]
    grad_two = (
        lax.dot_general(
            deriv_bf, scaled_rows, (((0,), (0,)), ((), ())), preferred_element_type=jnp.float32
        )
        * scales[1]
    )
    return (grad_one, grad_two, grad_three)


def third_sum(grad_three):
    return lax.psum(grad_three, ("row", "col"))


def shards(
    tensor,
    loss_kind,
    factor_one,
    factor_two,
    factor_three,
    first_one,
    second_one,
    first_two,
    second_two,
    first_three,
    second_three,
):
    tile_rows, tile_depth, tile_cols = tensor.shape
    full_rows = tile_rows * lax.axis_size("row")
    full_cols = tile_cols * lax.axis_size("col")
    scales = (
        1.0 / math.sqrt(full_cols * tile_depth),
        1.0 / math.sqrt(full_rows * tile_depth),
        1.0 / math.sqrt(full_rows * full_cols),
    )
    start_one, start_two, start_three = (factor_one, factor_two, factor_three)
    for iteration in range(ITERS):
        half_one = lax.all_gather(factor_one.astype(jnp.bfloat16), "col", axis=0, tiled=True)
        half_two = lax.all_gather(factor_two.astype(jnp.bfloat16), "row", axis=0, tiled=True)
        grad_one, grad_two, grad_three = tile_grads(
            tensor, loss_kind, half_one, half_two, factor_three.astype(jnp.bfloat16), scales
        )
        grad_one = lax.psum_scatter(grad_one, "col", scatter_dimension=0, tiled=True)
        grad_two = lax.psum_scatter(grad_two, "row", scatter_dimension=0, tiled=True)
        grad_three = third_sum(grad_three)
        counter = STEP + iteration + 1
        factor_one, first_one, second_one = adam_step(
            factor_one, first_one, second_one, grad_one, counter
        )
        factor_two, first_two, second_two = adam_step(
            factor_two, first_two, second_two, grad_two, counter
        )
        factor_three, first_three, second_three = adam_step(
            factor_three, first_three, second_three, grad_three, counter
        )
    spread = learn_rate * ITERS
    return (
        (start_one - factor_one) / spread,
        (start_two - factor_two) / spread,
        (start_three - factor_three) / spread,
    )


def solution(mesh):
    in_specs = (
        P("row", None, "col"),
        P("row", None, "col"),
        P(("row", "col"), None),
        P(("col", "row"), None),
        P(),
        P(("row", "col"), None),
        P(("row", "col"), None),
        P(("col", "row"), None),
        P(("col", "row"), None),
        P(),
        P(),
    )
    out_specs = (P(("row", "col"), None), P(("col", "row"), None), P())
    return jax.shard_map(shards, mesh=mesh, in_specs=in_specs, out_specs=out_specs, check_vma=False)
```

profile of v0, /device:TPU:0, one launch (start us, length us, event | category | flops | bytes accessed | tf_op | source)
XLA Modules:
  0.0 399.3 jit_solution(8798334853152890748)
XLA Ops:
  8.0 0.8 convert_element_type.63
  8.8 0.8 convert_element_type.57
  9.7 6.5 %all_gather.12 = bf16[128,512]{1,0:T(8,128)(2,1)S(1)} all-gather(bf16[32,512]{1,0:T(8,128)(2,1)S(1)} %convert_element_type.57), channel_id=1, replica_groups=mesh['row'=8,'col'=4] {'col'}, dimensions={0}, use_global_device_ids=true | all-gather | bytes 163840 | tf_op jit(solution)/shard_map/all_gather | solution.py:90
  16.1 31.3 %all_gather.13 = bf16[128,512]{1,0:T(8,128)(2,1)S(1)} all-gather(bf16[16,512]{1,0:T(8,128)(2,1)S(1)} %convert_element_type.63), channel_id=1, replica_groups=mesh['row'=8,'col'=4] {'row'}, dimensions={0}, use_global_device_ids=true | all-gather | bytes 147456 | tf_op jit(solution)/shard_map/all_gather | solution.py:91
  47.4 0.9 convert_convert_fusion
  48.3 2.8 broadcast_compare_fusion
  51.1 3.3 multiply_convert_fusion.1
  54.5 2.4 fusion.1
  56.9 0.8 copy-done.1
  57.7 8.1 %multiply_reduce_fusion.3 = (f32[128,512]{1,0:T(8,128)S(1)}, f32[8192,512]{1,0:T(8,128)}) fusion(f32[64,512]{1,0:T(8,128)S(1)} %convert_convert_fusion, bf16[8192,128]{1,0:T(8,128)(2,1)S(1)} %fusion.1, bf16[128,512]{1,0:T(8,128)(2,1)S(1)} %all_gather.13), kind=kOutput, calls=%fused_computation.4 | convolution fusion | flops 1082064896 | bytes 19398656 | tf_op jit(solution)/shard_map/dot_general | solution.py:49
  65.8 8.4 %multiply_reduce_fusion.2 = f32[64,512]{1,0:T(8,128)S(1)} fusion(f32[128,64,512]{2,1,0:T(8,128)} %bitcast.30, f32[128,512]{1,0:T(8,128)S(1)} %convert_element_type.58), kind=kLoop, calls=%fused_computation.3 | loop fusion | flops 8355840 | bytes 17170432 | tf_op jit(solution)/shard_map/reduce_sum | solution.py:53
  74.2 0.7 broadcast_multiply_fusion.3
  75.1 5.5 %convolution_multiply_fusion.1 = f32[128,512]{1,0:T(8,128)} fusion(bf16[8192,128]{1,0:T(8,128)(2,1)S(1)} %fusion.1, bf16[8192,512]{1,0:T(8,128)(2,1)} %bitcast.35), kind=kOutput, calls=%fused_computation.19 | convolution fusion | flops 1073807360 | bytes 10747904 | tf_op jit(solution)/shard_map/dot_general | solution.py:55
  80.7 0.7 broadcast_multiply_fusion.1
  81.5 119.0 %all-reduce.3.cloned.1.call-done = f32[64,512]{1,0:T(8,128)} async-done(((f32[64,512]{1,0:T(8,128)}), f32[64,512]{1,0:T(8,128)}) %all-reduce.3.cloned.1.call-update) | async-done | bytes 131088 | tf_op jit(solution)/shard_map/psum | solution.py:64
  200.5 1.0 fusion.24
  201.6 0.8 fusion.36
  202.4 30.5 %all_gather.15 = bf16[128,512]{1,0:T(8,128)(2,1)S(1)} all-gather(bf16[16,512]{1,0:T(8,128)(2,1)S(1)} %fusion.36), channel_id=1, replica_groups=mesh['row'=8,'col'=4] {'row'}, dimensions={0}, use_global_device_ids=true | all-gather | bytes 147456 | tf_op jit(solution)/shard_map/all_gather | solution.py:91
  232.9 0.9 fusion.26
  233.8 5.6 %all_gather.14 = bf16[128,512]{1,0:T(8,128)(2,1)S(1)} all-gather(bf16[32,512]{1,0:T(8,128)(2,1)S(1)} %fusion.26), channel_id=1, replica_groups=mesh['row'=8,'col'=4] {'col'}, dimensions={0}, use_global_device_ids=true | all-gather | bytes 163840 | tf_op jit(solution)/shard_map/all_gather | solution.py:90
  239.4 3.3 multiply_convert_fusion
  242.8 2.4 fusion.3
  245.2 0.8 copy-done
  246.0 8.1 %multiply_reduce_fusion.1 = (f32[128,512]{1,0:T(8,128)S(1)}, f32[8192,512]{1,0:T(8,128)}) fusion(f32[64,512]{1,0:T(8,128)S(1)} %fusion.24, bf16[8192,128]{1,0:T(8,128)(2,1)S(1)} %fusion.3, bf16[128,512]{1,0:T(8,128)(2,1)S(1)} %all_gather.15), kind=kOutput, calls=%fused_computation.1 | convolution fusion | flops 1082064896 | bytes 19398656 | tf_op jit(solution)/shard_map/dot_general | solution.py:49
  254.1 8.4 %multiply_reduce_fusion = f32[64,512]{1,0:T(8,128)S(1)} fusion(f32[128,64,512]{2,1,0:T(8,128)} %bitcast.31, f32[128,512]{1,0:T(8,128)S(1)} %convert_element_type.68), kind=kLoop, calls=%fused_computation | loop fusion | flops 8355840 | bytes 17170432 | tf_op jit(solution)/shard_map/reduce_sum | solution.py:53
  262.5 0.7 broadcast_multiply_fusion.2
  263.3 5.4 %convolution_multiply_fusion = f32[128,512]{1,0:T(8,128)} fusion(bf16[8192,128]{1,0:T(8,128)(2,1)S(1)} %fusion.3, bf16[8192,512]{1,0:T(8,128)(2,1)} %bitcast.33), kind=kOutput, calls=%fused_computation.18 | convolution fusion | flops 1073807360 | bytes 10747904 | tf_op jit(solution)/shard_map/dot_general | solution.py:55
  268.8 0.7 broadcast_multiply_fusion
  269.5 117.4 %all-reduce.5.cloned.1.call-done = f32[64,512]{1,0:T(8,128)} async-done(((f32[64,512]{1,0:T(8,128)}), f32[64,512]{1,0:T(8,128)}) %all-reduce.5.cloned.1.call-update) | async-done | bytes 131088 | tf_op jit(solution)/shard_map/psum | solution.py:64
  386.9 1.7 fusion.14
  388.7 1.4 fusion.35
  390.1 1.6 fusion.25
  (54 shorter events, 0.5 us)
Async XLA Ops:
  8.0 192.5 %all-reduce.3.cloned.1.call-start = ((), (), s32[]{:S(2)}) async-start(), calls=%async_computation.5 | async-start | bytes 262144 | tf_op jit(solution)/shard_map/psum | solution.py:64
  51.1 3.4 copy-start.3
  51.1 3.4 copy-start.17
  54.5 3.2 copy-start.1
  74.9 125.6 %copy-start.2 = (f32[64,512]{1,0:T(8,128)S(1)}, f32[64,512]{1,0:T(8,128)}, u32[]{:S(2)}) copy-start(f32[64,512]{1,0:T(8,128)} %param.15) | copy-start | bytes 393220
  74.9 125.6 %copy-start.6 = (f32[64,512]{1,0:T(8,128)S(1)}, f32[64,512]{1,0:T(8,128)}, u32[]{:S(2)}) copy-start(f32[64,512]{1,0:T(8,128)} %param.20) | copy-start | bytes 393220
  74.9 125.6 %copy-start.7 = (f32[64,512]{1,0:T(8,128)S(1)}, f32[64,512]{1,0:T(8,128)}, u32[]{:S(2)}) copy-start(f32[64,512]{1,0:T(8,128)} %param.21) | copy-start | bytes 393220
  74.9 126.6 %copy-start.9 = (f32[16,512]{1,0:T(8,128)S(1)}, f32[16,512]{1,0:T(8,128)}, u32[]{:S(2)}) copy-start(f32[16,512]{1,0:T(8,128)} %param.14) | copy-start | bytes 98308
  75.0 126.6 %copy-start.13 = (f32[16,512]{1,0:T(8,128)S(1)}, f32[16,512]{1,0:T(8,128)}, u32[]{:S(2)}) copy-start(f32[16,512]{1,0:T(8,128)} %param.18) | copy-start | bytes 98308
  75.0 126.6 %copy-start.14 = (f32[16,512]{1,0:T(8,128)S(1)}, f32[16,512]{1,0:T(8,128)}, u32[]{:S(2)}) copy-start(f32[16,512]{1,0:T(8,128)} %param.19) | copy-start | bytes 98308
  75.0 157.9 %copy-start.5 = (f32[32,512]{1,0:T(8,128)S(1)}, f32[32,512]{1,0:T(8,128)}, u32[]{:S(2)}) copy-start(f32[32,512]{1,0:T(8,128)} %param.13) | copy-start | bytes 196612
  75.0 157.9 %copy-start.10 = (f32[32,512]{1,0:T(8,128)S(1)}, f32[32,512]{1,0:T(8,128)}, u32[]{:S(2)}) copy-start(f32[32,512]{1,0:T(8,128)} %param.16) | copy-start | bytes 196612
  75.0 157.9 %copy-start.11 = (f32[32,512]{1,0:T(8,128)S(1)}, f32[32,512]{1,0:T(8,128)}, u32[]{:S(2)}) copy-start(f32[32,512]{1,0:T(8,128)} %param.17) | copy-start | bytes 196612
  75.0 126.5 %reduce-scatter.7.cloned.1.call-start = ((), (), s32[]{:S(2)}) async-start(), calls=%async_computation.6 | async-start | bytes 294912 | tf_op jit(solution)/shard_map/reduce_scatter | solution.py:96
  80.6 152.3 %reduce-scatter.5.cloned.1.call-start = ((), (), s32[]{:S(2)}) async-start(), calls=%async_computation.4 | async-start | bytes 327680 | tf_op jit(solution)/shard_map/reduce_scatter | solution.py:95
  81.4 305.5 %all-reduce.5.cloned.1.call-start = ((), (), s32[]{:S(2)}) async-start(), calls=%async_computation.9 | async-start | bytes 262144 | tf_op jit(solution)/shard_map/psum | solution.py:64
  239.4 3.4 copy-start.4
  239.4 3.4 copy-start.18
  242.8 3.2 copy-start
  263.2 123.7 %copy-start.8 = (f32[64,512]{1,0:T(8,128)S(1)}, f32[64,512]{1,0:T(8,128)}, u32[]{:S(2)}) copy-start(f32[64,512]{1,0:T(8,128)} %all-reduce.3.cloned.1.call-done) | copy-start | bytes 393220
  263.2 125.5 %copy-start.15 = (f32[16,512]{1,0:T(8,128)S(1)}, f32[16,512]{1,0:T(8,128)}, u32[]{:S(2)}) copy-start(f32[16,512]{1,0:T(8,128)} %param.19) | copy-start | bytes 98308
  263.2 125.5 %copy-start.16 = (f32[16,512]{1,0:T(8,128)S(1)}, f32[16,512]{1,0:T(8,128)}, u32[]{:S(2)}) copy-start(f32[16,512]{1,0:T(8,128)} %reduce-scatter.7.cloned.1.call-done) | copy-start | bytes 98308
  263.2 126.9 %copy-start.12 = (f32[32,512]{1,0:T(8,128)S(1)}, f32[32,512]{1,0:T(8,128)}, u32[]{:S(2)}) copy-start(f32[32,512]{1,0:T(8,128)} %reduce-scatter.5.cloned.1.call-done) | copy-start | bytes 196612
  263.2 125.4 %reduce-scatter.11.cloned.1.call-start = ((), (), s32[]{:S(2)}) async-start(), calls=%async_computation.8 | async-start | bytes 294912 | tf_op jit(solution)/shard_map/reduce_scatter | solution.py:96
  268.7 121.4 %reduce-scatter.9.cloned.1.call-start = ((), (), s32[]{:S(2)}) async-start(), calls=%async_computation.7 | async-start | bytes 327680 | tf_op jit(solution)/shard_map/reduce_scatter | solution.py:95
Sparse Core Ops, SparseCore 0:
  75.0 125.4 all-reduce.2
  263.3 123.5 all-reduce.4
Sparse Core Ops, SparseCore 1:
  80.7 63.0 reduce-scatter.6
  146.1 19.0 reduce-scatter.4
  268.8 61.1 reduce-scatter.10
  332.5 19.0 reduce-scatter.8
where the time goes:
time: 400 us; the launch traced here: 399 us
  waiting for transfers between devices  237 us (59%)
  blocking collectives  73.9 us (18%)
  other arithmetic  39.1 us (10%)
  matrix products  31.8 us (8%)
  between operations  16 us (4%)
    psum x2, waiting for transfers between devices, third_sum(): return lax.psum(grad_three, ('row', 'col'))  236 us
    all_gather x2, blocking collectives, shards(): lax.all_gather(factor_two.astype(jnp.bfloat16), 'row', axis=0, tiled=True)  61.8 us
    reduce_sum x2, other arithmetic, tile_grads(): grad_three = jnp.sum(projected * one_f[:, None, :], axis=0) * scales[2]  16.8 us
    dot_general x2, matrix products, tile_grads(): jnp.dot(deriv_bf, half_two, preferred_element_type=jnp.float32)  16.2 us
    all_gather x2, blocking collectives, shards(): lax.all_gather(factor_one.astype(jnp.bfloat16), 'col', axis=0, tiled=True)  12.1 us
    dot_general x2, matrix products, tile_grads(): lax.dot_general(deriv_bf, scaled_rows, (((0,), (0,)), ((), ())), preferre...  10.9 us
  transfers between devices with their start and end apart: 6, of which 2 were waited for; matrix products, arithmetic and copies ran while one was open for 4% of the time, Pallas kernels for 0%

commit v1 on v0

--- a/solution.py
+++ b/solution.py
@@ -88,7 +88,17 @@
     start_one, start_two, start_three = (factor_one, factor_two, factor_three)
     for iteration in range(ITERS):
         half_one = lax.all_gather(factor_one.astype(jnp.bfloat16), "col", axis=0, tiled=True)
-        half_two = lax.all_gather(factor_two.astype(jnp.bfloat16), "row", axis=0, tiled=True)
+        x = factor_two.astype(jnp.bfloat16)
+        ways = lax.axis_size("row")
+        up = [(d, (d + 1) % ways) for d in range(ways)]
+        down = [(d, (d - 1) % ways) for d in range(ways)]
+        earlier, later = ([x], [x])
+        for _ in range(ways // 2):
+            earlier.append(lax.ppermute(earlier[-1], "row", up))
+        for _ in range((ways - 1) // 2):
+            later.append(lax.ppermute(later[-1], "row", down))
+        line = jnp.concatenate([*earlier[::-1], *later[1:]], axis=0)
+        half_two = jnp.roll(line, (lax.axis_index("row") - ways // 2) * x.shape[0], axis=0)
         grad_one, grad_two, grad_three = tile_grads(
             tensor, loss_kind, half_one, half_two, factor_three.astype(jnp.bfloat16), scales
         )

time: 400 us -> 388 us (0.970)
  blocking collectives: 73.9 us -> 10.8 us
  starting transfers between devices: 0.25 us -> 30.8 us
  waiting for transfers between devices: 237 us -> 256 us
    all_gather x2 -> x0, blocking collectives: 61.8 us -> none  [shards(): lax.all_gather(factor_two.astype(jnp.bfloat16), 'row', axis=0, tiled=True)]
    reduce_scatter x2, waiting for transfers between devices: 0.03 us -> 53.5 us  [shards(): lax.psum_scatter(grad_two, 'row', scatter_dimension=0, tiled=True)]
    psum x2, waiting for transfers between devices: 236 us -> 188 us  [third_sum(): return lax.psum(grad_three, ('row', 'col'))]
    ppermute x0 -> x14, starting transfers between devices: none -> 30.3 us  [the longest x6 28.8 us: shards(): later.append(lax.ppermute(later[-1], 'row', down))]
    ppermute x0 -> x14, waiting for transfers between devices: none -> 14.7 us  [the longest x8 11.2 us: shards(): earlier.append(lax.ppermute(earlier[-1], 'row', up))]
    dot_general x2, matrix products: 4.74 us -> 9.01 us  [tile_grads(): lax.dot_general(scaled_rows, half_two, (((1,), (1,)), ((), ())), preferre...]
  transfers between devices with their start and end apart: 6 -> 20, of which waited for: 2 -> 9; matrix products, arithmetic and copies ran while one was open for 4% -> 9% of each run, Pallas kernels for 0% -> 0%
where the time goes in v1:
time: 388 us; the launch traced here: 387 us
  waiting for transfers between devices  256 us (66%)
  other arithmetic  40.2 us (10%)
  matrix products  33.7 us (9%)
  starting transfers between devices  30.8 us (8%)
  between operations  15.6 us (4%)
  blocking collectives  10.8 us (3%)
    psum x2, waiting for transfers between devices, third_sum(): return lax.psum(grad_three, ('row', 'col'))  188 us
    reduce_scatter x2, waiting for transfers between devices, shards(): lax.psum_scatter(grad_two, 'row', scatter_dimension=0, tiled=True)  53.5 us
    ppermute x6, starting transfers between devices, shards(): later.append(lax.ppermute(later[-1], 'row', down))  28.8 us
    dot_general x2, matrix products, tile_grads(): jnp.dot(deriv_bf, half_two, preferred_element_type=jnp.float32)  17.2 us
    reduce_sum x2, other arithmetic, tile_grads(): grad_three = jnp.sum(projected * one_f[:, None, :], axis=0) * scales[2]  17 us
    ppermute x8, waiting for transfers between devices, shards(): earlier.append(lax.ppermute(earlier[-1], 'row', up))  11.2 us
    all_gather x2, blocking collectives, shards(): lax.all_gather(factor_one.astype(jnp.bfloat16), 'col', axis=0, tiled=True)  10.8 us
    convert_element_type x2, other arithmetic, tile_grads(): scaled_rows = (one_f[:, None, :] * three_f[None, :, :]).astype(jnp.bfloat...  9.85 us
  transfers between devices with their start and end apart: 20, of which 9 were waited for; matrix products, arithmetic and copies ran while one was open for 9% of the time, Pallas kernels for 0%

profile of v1, /device:TPU:0, one launch (start us, length us, event | category | flops | bytes accessed | tf_op | source)
XLA Modules:
  0.0 387.4 jit_solution(4437035175513439434)
XLA Ops:
  8.8 6.0 %collective-permute-start.4 = (bf16[16,512]{1,0:T(8,128)(2,1)S(1)}, bf16[16,512]{1,0:T(8,128)(2,1)S(1)}, u32[]{:S(2)}, u32[]{:S(2)}) collective-permute-start(bf16[16,512]{1,0:T(8,128)(2,1)S(1)} %convert_element_type.63), channel_id=1, source_target_pairs={{0,28},{4,0},{8,4},{12,8},{16,12},{20,16},{24,20},{28,24},{1,29},{... | collective-permute-start | bytes 49160 | tf_op jit(solution)/shard_map/ppermute | solution.py:99
  14.8 0.9 convert_convert_fusion
  16.6 4.7 %collective-permute-done = bf16[16,512]{1,0:T(8,128)(2,1)S(1)} collective-permute-done((bf16[16,512]{1,0:T(8,128)(2,1)S(1)}, bf16[16,512]{1,0:T(8,128)(2,1)S(1)}, u32[]{:S(2)}, u32[]{:S(2)}) %collective-permute-start) | collective-permute-done | bytes 16416 | tf_op jit(solution)/shard_map/ppermute | solution.py:97
  21.3 5.4 %all_gather.6 = bf16[128,512]{1,0:T(8,128)(2,1)S(1)} all-gather(bf16[32,512]{1,0:T(8,128)(2,1)S(1)} %convert_element_type.57), channel_id=1, replica_groups=mesh['row'=8,'col'=4] {'col'}, dimensions={0}, use_global_device_ids=true | all-gather | bytes 163840 | tf_op jit(solution)/shard_map/all_gather | solution.py:90
  26.7 1.0 collective-permute-done.1
  27.7 6.5 %multiply_convert_fusion.1 = bf16[128,64,512]{2,1,0:T(8,128)(2,1)} fusion(f32[64,512]{1,0:T(8,128)S(1)} %convert_convert_fusion, f32[128,512]{1,0:T(8,128)S(1)} %convert_element_type.58), kind=kLoop, calls=%fused_computation.5 | loop fusion | flops 8388608 | bytes 8781824 | tf_op jit(solution)/shard_map/convert_element_type | solution.py:39
  34.2 4.7 %collective-permute-start.5 = (bf16[16,512]{1,0:T(8,128)(2,1)S(1)}, bf16[16,512]{1,0:T(8,128)(2,1)S(1)}, u32[]{:S(2)}, u32[]{:S(2)}) collective-permute-start(bf16[16,512]{1,0:T(8,128)(2,1)S(1)} %collective-permute-done.4), channel_id=1, source_target_pairs={{0,28},{4,0},{8,4},{12,8},{16,12},{20,16},{24,20},{28,24},{1,29},{... | collective-permute-start | bytes 49160 | tf_op jit(solution)/shard_map/ppermute | solution.py:99
  40.4 5.0 %collective-permute-start.6 = (bf16[16,512]{1,0:T(8,128)(2,1)S(1)}, bf16[16,512]{1,0:T(8,128)(2,1)S(1)}, u32[]{:S(2)}, u32[]{:S(2)}) collective-permute-start(bf16[16,512]{1,0:T(8,128)(2,1)S(1)} %collective-permute-done.5), channel_id=1, source_target_pairs={{0,28},{4,0},{8,4},{12,8},{16,12},{20,16},{24,20},{28,24},{1,29},{... | collective-permute-start | bytes 49160 | tf_op jit(solution)/shard_map/ppermute | solution.py:99
  45.5 1.4 collective-permute-done.6
  46.9 6.6 %fusion.1 = bf16[8192,128]{1,0:T(8,128)(2,1)S(1)} fusion(pred[128,64,128]{2,1,0:T(32,128)(4,1)S(1)} %broadcast_compare_fusion, bf16[128,64,128]{2,1,0:T(8,128)(2,1)} %param.13, bf16[8192,512]{1,0:T(8,128)(2,1)} %bitcast.28, s32[]{:T(128)S(6)} %select_n.28, bf16[128,512]{1,0:T(8,128)(2,1)S(1)} %constant_dynamic-update-slice_fusion), kind=kOutput, calls=%fused_computation.12 | convolution fusion | flops 1085538304 | bytes 13762564 | tf_op jit(solution)/shard_map/dot_general | solution.py:42
  53.4 2.1 convolution_multiply_fusion.1
  55.6 9.0 %multiply_reduce_fusion.3 = (f32[128,512]{1,0:T(8,128)S(1)}, f32[8192,512]{1,0:T(8,128)}) fusion(f32[64,512]{1,0:T(8,128)S(1)} %convert_convert_fusion, bf16[8192,128]{1,0:T(8,128)(2,1)S(1)} %fusion.1, s32[]{:T(128)S(6)} %select_n.28, bf16[128,512]{1,0:T(8,128)(2,1)} %copy-done.15), kind=kOutput, calls=%fused_computation.4 | convolution fusion | flops 1082327040 | bytes 19398660 | tf_op jit(solution)/shard_map/dot_general | solution.py:49
  64.9 8.5 %multiply_reduce_fusion.2 = f32[64,512]{1,0:T(8,128)S(1)} fusion(f32[128,64,512]{2,1,0:T(8,128)} %bitcast.26, f32[128,512]{1,0:T(8,128)S(1)} %convert_element_type.58), kind=kLoop, calls=%fused_computation.3 | loop fusion | flops 8355840 | bytes 17170432 | tf_op jit(solution)/shard_map/reduce_sum | solution.py:53
  75.0 53.5 %reduce-scatter.7.cloned.1.call-done = f32[16,512]{1,0:T(8,128)} async-done(((f32[128,512]{1,0:T(8,128)}), f32[16,512]{1,0:T(8,128)}) %reduce-scatter.7.cloned.1.call-update) | async-done | bytes 32784 | tf_op jit(solution)/shard_map/reduce_scatter | solution.py:106
  129.3 1.5 collective-permute-start.7
  130.8 69.2 %all-reduce.3.cloned.1.call-done = f32[64,512]{1,0:T(8,128)} async-done(((f32[64,512]{1,0:T(8,128)}), f32[64,512]{1,0:T(8,128)}) %all-reduce.3.cloned.1.call-update) | async-done | bytes 131088 | tf_op jit(solution)/shard_map/psum | solution.py:64
  200.0 1.0 fusion.26
  201.0 3.3 collective-permute-start.11
  205.3 5.5 %collective-permute-done.8 = bf16[16,512]{1,0:T(8,128)(2,1)S(1)} collective-permute-done((bf16[16,512]{1,0:T(8,128)(2,1)S(1)}, bf16[16,512]{1,0:T(8,128)(2,1)S(1)}, u32[]{:S(2)}, u32[]{:S(2)}) %collective-permute-start.8) | collective-permute-done | bytes 16416 | tf_op jit(solution)/shard_map/ppermute | solution.py:97
  210.8 5.4 %all_gather.7 = bf16[128,512]{1,0:T(8,128)(2,1)S(1)} all-gather(bf16[32,512]{1,0:T(8,128)(2,1)S(1)} %fusion.28), channel_id=1, replica_groups=mesh['row'=8,'col'=4] {'col'}, dimensions={0}, use_global_device_ids=true | all-gather | bytes 163840 | tf_op jit(solution)/shard_map/all_gather | solution.py:90
  216.3 4.8 %collective-permute-start.12 = (bf16[16,512]{1,0:T(8,128)(2,1)S(1)}, bf16[16,512]{1,0:T(8,128)(2,1)S(1)}, u32[]{:S(2)}, u32[]{:S(2)}) collective-permute-start(bf16[16,512]{1,0:T(8,128)(2,1)S(1)} %collective-permute-done.11), channel_id=1, source_target_pairs={{0,28},{4,0},{8,4},{12,8},{16,12},{20,16},{24,20},{28,24},{1,29},{... | collective-permute-start | bytes 49160 | tf_op jit(solution)/shard_map/ppermute | solution.py:99
  221.0 3.3 multiply_convert_fusion
  224.4 5.0 %collective-permute-start.13 = (bf16[16,512]{1,0:T(8,128)(2,1)S(1)}, bf16[16,512]{1,0:T(8,128)(2,1)S(1)}, u32[]{:S(2)}, u32[]{:S(2)}) collective-permute-start(bf16[16,512]{1,0:T(8,128)(2,1)S(1)} %collective-permute-done.12), channel_id=1, source_target_pairs={{0,28},{4,0},{8,4},{12,8},{16,12},{20,16},{24,20},{28,24},{1,29},{... | collective-permute-start | bytes 49160 | tf_op jit(solution)/shard_map/ppermute | solution.py:99
  229.5 1.4 collective-permute-done.13
  230.8 2.5 fusion.3
  233.3 8.2 %multiply_reduce_fusion.1 = (f32[128,512]{1,0:T(8,128)S(1)}, f32[8192,512]{1,0:T(8,128)}) fusion(f32[64,512]{1,0:T(8,128)S(1)} %fusion.26, bf16[8192,128]{1,0:T(8,128)(2,1)S(1)} %fusion.3, s32[]{:T(128)S(6)} %select_n.28, bf16[128,512]{1,0:T(8,128)(2,1)S(1)} %constant_dynamic-update-slice_fusion.8), kind=kOutput, calls=%fused_computation.1 | convolution fusion | flops 1082327040 | bytes 19398660 | tf_op jit(solution)/shard_map/dot_general | solution.py:49
  241.5 8.4 %multiply_reduce_fusion = f32[64,512]{1,0:T(8,128)S(1)} fusion(f32[128,64,512]{2,1,0:T(8,128)} %bitcast.27, f32[128,512]{1,0:T(8,128)S(1)} %convert_element_type.68), kind=kLoop, calls=%fused_computation | loop fusion | flops 8355840 | bytes 17170432 | tf_op jit(solution)/shard_map/reduce_sum | solution.py:53
  250.7 5.4 %convolution_multiply_fusion = f32[128,512]{1,0:T(8,128)} fusion(bf16[8192,128]{1,0:T(8,128)(2,1)S(1)} %fusion.3, bf16[8192,512]{1,0:T(8,128)(2,1)} %bitcast.31), kind=kOutput, calls=%fused_computation.18 | convolution fusion | flops 1073807360 | bytes 10747904 | tf_op jit(solution)/shard_map/dot_general | solution.py:55
  257.0 118.6 %all-reduce.5.cloned.1.call-done = f32[64,512]{1,0:T(8,128)} async-done(((f32[64,512]{1,0:T(8,128)}), f32[64,512]{1,0:T(8,128)}) %all-reduce.5.cloned.1.call-update) | async-done | bytes 131088 | tf_op jit(solution)/shard_map/psum | solution.py:64
  375.6 1.7 fusion.16
  377.3 1.4 fusion.37
  378.8 1.6 fusion.27
  (98 shorter events, 8.3 us)
Async XLA Ops:
  8.0 120.5 %reduce-scatter.7.cloned.1.call-start = ((), (), s32[]{:S(2)}) async-start(), calls=%async_computation.6 | async-start | bytes 294912 | tf_op jit(solution)/shard_map/reduce_scatter | solution.py:106
  8.8 25.4 %collective-permute-start.4 = (bf16[16,512]{1,0:T(8,128)(2,1)S(1)}, bf16[16,512]{1,0:T(8,128)(2,1)S(1)}, u32[]{:S(2)}, u32[]{:S(2)}) collective-permute-start(bf16[16,512]{1,0:T(8,128)(2,1)S(1)} %convert_element_type.63), channel_id=1, source_target_pairs={{0,28},{4,0},{8,4},{12,8},{16,12},{20,16},{24,20},{28,24},{1,29},{... | collective-permute-start | bytes 49160 | tf_op jit(solution)/shard_map/ppermute | solution.py:99
  14.8 6.4 %collective-permute-start = (bf16[16,512]{1,0:T(8,128)(2,1)S(1)}, bf16[16,512]{1,0:T(8,128)(2,1)S(1)}, u32[]{:S(2)}, u32[]{:S(2)}) collective-permute-start(bf16[16,512]{1,0:T(8,128)(2,1)S(1)} %convert_element_type.63), channel_id=1, source_target_pairs={{0,4},{4,8},{8,12},{12,16},{16,20},{20,24},{24,28},{28,0},{1,5},{5... | collective-permute-start | bytes 49160 | tf_op jit(solution)/shard_map/ppermute | solution.py:97
  21.3 6.4 %collective-permute-start.1 = (bf16[16,512]{1,0:T(8,128)(2,1)S(1)}, bf16[16,512]{1,0:T(8,128)(2,1)S(1)}, u32[]{:S(2)}, u32[]{:S(2)}) collective-permute-start(bf16[16,512]{1,0:T(8,128)(2,1)S(1)} %collective-permute-done), channel_id=1, source_target_pairs={{0,4},{4,8},{8,12},{12,16},{16,20},{20,24},{24,28},{28,0},{1,5},{5... | collective-permute-start | bytes 49160 | tf_op jit(solution)/shard_map/ppermute | solution.py:97
  27.7 11.3 %collective-permute-start.2 = (bf16[16,512]{1,0:T(8,128)(2,1)S(1)}, bf16[16,512]{1,0:T(8,128)(2,1)S(1)}, u32[]{:S(2)}, u32[]{:S(2)}) collective-permute-start(bf16[16,512]{1,0:T(8,128)(2,1)S(1)} %collective-permute-done.1), channel_id=1, source_target_pairs={{0,4},{4,8},{8,12},{12,16},{16,20},{20,24},{24,28},{28,0},{1,5},{5... | collective-permute-start | bytes 49160 | tf_op jit(solution)/shard_map/ppermute | solution.py:97
  34.2 6.2 %collective-permute-start.5 = (bf16[16,512]{1,0:T(8,128)(2,1)S(1)}, bf16[16,512]{1,0:T(8,128)(2,1)S(1)}, u32[]{:S(2)}, u32[]{:S(2)}) collective-permute-start(bf16[16,512]{1,0:T(8,128)(2,1)S(1)} %collective-permute-done.4), channel_id=1, source_target_pairs={{0,28},{4,0},{8,4},{12,8},{16,12},{20,16},{24,20},{28,24},{1,29},{... | collective-permute-start | bytes 49160 | tf_op jit(solution)/shard_map/ppermute | solution.py:99
  39.0 6.4 %collective-permute-start.3 = (bf16[16,512]{1,0:T(8,128)(2,1)S(1)}, bf16[16,512]{1,0:T(8,128)(2,1)S(1)}, u32[]{:S(2)}, u32[]{:S(2)}) collective-permute-start(bf16[16,512]{1,0:T(8,128)(2,1)S(1)} %collective-permute-done.2), channel_id=1, source_target_pairs={{0,4},{4,8},{8,12},{12,16},{16,20},{20,24},{24,28},{28,0},{1,5},{5... | collective-permute-start | bytes 49160 | tf_op jit(solution)/shard_map/ppermute | solution.py:97
  40.4 6.4 %collective-permute-start.6 = (bf16[16,512]{1,0:T(8,128)(2,1)S(1)}, bf16[16,512]{1,0:T(8,128)(2,1)S(1)}, u32[]{:S(2)}, u32[]{:S(2)}) collective-permute-start(bf16[16,512]{1,0:T(8,128)(2,1)S(1)} %collective-permute-done.5), channel_id=1, source_target_pairs={{0,28},{4,0},{8,4},{12,8},{16,12},{20,16},{24,20},{28,24},{1,29},{... | collective-permute-start | bytes 49160 | tf_op jit(solution)/shard_map/ppermute | solution.py:99
  64.6 135.5 %all-reduce.3.cloned.1.call-start = ((), (), s32[]{:S(2)}) async-start(), calls=%async_computation.5 | async-start | bytes 262144 | tf_op jit(solution)/shard_map/psum | solution.py:64
  64.8 63.7 %copy-start.11 = (f32[16,512]{1,0:T(8,128)S(1)}, f32[16,512]{1,0:T(8,128)}, u32[]{:S(2)}) copy-start(f32[16,512]{1,0:T(8,128)} %param.16) | copy-start | bytes 98308
  64.8 63.7 %copy-start.16 = (f32[16,512]{1,0:T(8,128)S(1)}, f32[16,512]{1,0:T(8,128)}, u32[]{:S(2)}) copy-start(f32[16,512]{1,0:T(8,128)} %param.20) | copy-start | bytes 98308
  64.8 63.7 %copy-start.17 = (f32[16,512]{1,0:T(8,128)S(1)}, f32[16,512]{1,0:T(8,128)}, u32[]{:S(2)}) copy-start(f32[16,512]{1,0:T(8,128)} %param.21) | copy-start | bytes 98308
  64.8 135.2 %copy-start.3 = (f32[64,512]{1,0:T(8,128)S(1)}, f32[64,512]{1,0:T(8,128)}, u32[]{:S(2)}) copy-start(f32[64,512]{1,0:T(8,128)} %param.17) | copy-start | bytes 393220
  64.9 135.2 %copy-start.7 = (f32[64,512]{1,0:T(8,128)S(1)}, f32[64,512]{1,0:T(8,128)}, u32[]{:S(2)}) copy-start(f32[64,512]{1,0:T(8,128)} %param.22) | copy-start | bytes 393220
  64.9 135.2 %copy-start.8 = (f32[64,512]{1,0:T(8,128)S(1)}, f32[64,512]{1,0:T(8,128)}, u32[]{:S(2)}) copy-start(f32[64,512]{1,0:T(8,128)} %param.23) | copy-start | bytes 393220
  64.9 139.5 %copy-start.6 = (f32[32,512]{1,0:T(8,128)S(1)}, f32[32,512]{1,0:T(8,128)}, u32[]{:S(2)}) copy-start(f32[32,512]{1,0:T(8,128)} %param.15) | copy-start | bytes 196612
  64.9 139.5 %copy-start.12 = (f32[32,512]{1,0:T(8,128)S(1)}, f32[32,512]{1,0:T(8,128)}, u32[]{:S(2)}) copy-start(f32[32,512]{1,0:T(8,128)} %param.18) | copy-start | bytes 196612
  64.9 139.5 %copy-start.13 = (f32[32,512]{1,0:T(8,128)S(1)}, f32[32,512]{1,0:T(8,128)}, u32[]{:S(2)}) copy-start(f32[32,512]{1,0:T(8,128)} %param.19) | copy-start | bytes 196612
  74.2 130.2 %reduce-scatter.5.cloned.1.call-start = ((), (), s32[]{:S(2)}) async-start(), calls=%async_computation.4 | async-start | bytes 327680 | tf_op jit(solution)/shard_map/reduce_scatter | solution.py:105
  75.0 300.6 %all-reduce.5.cloned.1.call-start = ((), (), s32[]{:S(2)}) async-start(), calls=%async_computation.9 | async-start | bytes 262144 | tf_op jit(solution)/shard_map/psum | solution.py:64
  129.3 75.1 %collective-permute-start.7 = (bf16[16,512]{1,0:T(8,128)(2,1)S(1)}, bf16[16,512]{1,0:T(8,128)(2,1)S(1)}, u32[]{:S(2)}, u32[]{:S(2)}) collective-permute-start(bf16[16,512]{1,0:T(8,128)(2,1)S(1)} %fusion.38), channel_id=1, source_target_pairs={{0,4},{4,8},{8,12},{12,16},{16,20},{20,24},{24,28},{28,0},{1,5},{5... | collective-permute-start | bytes 49160 | tf_op jit(solution)/shard_map/ppermute | solution.py:97
  201.0 15.2 %collective-permute-start.11 = (bf16[16,512]{1,0:T(8,128)(2,1)S(1)}, bf16[16,512]{1,0:T(8,128)(2,1)S(1)}, u32[]{:S(2)}, u32[]{:S(2)}) collective-permute-start(bf16[16,512]{1,0:T(8,128)(2,1)S(1)} %fusion.38), channel_id=1, source_target_pairs={{0,28},{4,0},{8,4},{12,8},{16,12},{20,16},{24,20},{28,24},{1,29},{... | collective-permute-start | bytes 49160 | tf_op jit(solution)/shard_map/ppermute | solution.py:99
  204.4 6.4 %collective-permute-start.8 = (bf16[16,512]{1,0:T(8,128)(2,1)S(1)}, bf16[16,512]{1,0:T(8,128)(2,1)S(1)}, u32[]{:S(2)}, u32[]{:S(2)}) collective-permute-start(bf16[16,512]{1,0:T(8,128)(2,1)S(1)} %collective-permute-done.7), channel_id=1, source_target_pairs={{0,4},{4,8},{8,12},{12,16},{16,20},{20,24},{24,28},{28,0},{1,5},{5... | collective-permute-start | bytes 49160 | tf_op jit(solution)/shard_map/ppermute | solution.py:97
  210.8 10.2 %collective-permute-start.9 = (bf16[16,512]{1,0:T(8,128)(2,1)S(1)}, bf16[16,512]{1,0:T(8,128)(2,1)S(1)}, u32[]{:S(2)}, u32[]{:S(2)}) collective-permute-start(bf16[16,512]{1,0:T(8,128)(2,1)S(1)} %collective-permute-done.8), channel_id=1, source_target_pairs={{0,4},{4,8},{8,12},{12,16},{16,20},{20,24},{24,28},{28,0},{1,5},{5... | collective-permute-start | bytes 49160 | tf_op jit(solution)/shard_map/ppermute | solution.py:97
  216.3 8.1 %collective-permute-start.12 = (bf16[16,512]{1,0:T(8,128)(2,1)S(1)}, bf16[16,512]{1,0:T(8,128)(2,1)S(1)}, u32[]{:S(2)}, u32[]{:S(2)}) collective-permute-start(bf16[16,512]{1,0:T(8,128)(2,1)S(1)} %collective-permute-done.11), channel_id=1, source_target_pairs={{0,28},{4,0},{8,4},{12,8},{16,12},{20,16},{24,20},{28,24},{1,29},{... | collective-permute-start | bytes 49160 | tf_op jit(solution)/shard_map/ppermute | solution.py:99
  221.0 8.4 %collective-permute-start.10 = (bf16[16,512]{1,0:T(8,128)(2,1)S(1)}, bf16[16,512]{1,0:T(8,128)(2,1)S(1)}, u32[]{:S(2)}, u32[]{:S(2)}) collective-permute-start(bf16[16,512]{1,0:T(8,128)(2,1)S(1)} %collective-permute-done.9), channel_id=1, source_target_pairs={{0,4},{4,8},{8,12},{12,16},{16,20},{20,24},{24,28},{28,0},{1,5},{5... | collective-permute-start | bytes 49160 | tf_op jit(solution)/shard_map/ppermute | solution.py:97
  224.4 6.4 %collective-permute-start.13 = (bf16[16,512]{1,0:T(8,128)(2,1)S(1)}, bf16[16,512]{1,0:T(8,128)(2,1)S(1)}, u32[]{:S(2)}, u32[]{:S(2)}) collective-permute-start(bf16[16,512]{1,0:T(8,128)(2,1)S(1)} %collective-permute-done.12), channel_id=1, source_target_pairs={{0,28},{4,0},{8,4},{12,8},{16,12},{20,16},{24,20},{28,24},{1,29},{... | collective-permute-start | bytes 49160 | tf_op jit(solution)/shard_map/ppermute | solution.py:99
  250.6 124.9 %copy-start.9 = (f32[64,512]{1,0:T(8,128)S(1)}, f32[64,512]{1,0:T(8,128)}, u32[]{:S(2)}) copy-start(f32[64,512]{1,0:T(8,128)} %all-reduce.3.cloned.1.call-done) | copy-start | bytes 393220
  250.6 126.7 %copy-start.18 = (f32[16,512]{1,0:T(8,128)S(1)}, f32[16,512]{1,0:T(8,128)}, u32[]{:S(2)}) copy-start(f32[16,512]{1,0:T(8,128)} %reduce-scatter.7.cloned.1.call-done) | copy-start | bytes 98308
  250.6 128.1 %copy-start.14 = (f32[32,512]{1,0:T(8,128)S(1)}, f32[32,512]{1,0:T(8,128)}, u32[]{:S(2)}) copy-start(f32[32,512]{1,0:T(8,128)} %reduce-scatter.5.cloned.1.call-done) | copy-start | bytes 196612
  250.7 126.7 %reduce-scatter.11.cloned.1.call-start = ((), (), s32[]{:S(2)}) async-start(), calls=%async_computation.8 | async-start | bytes 294912 | tf_op jit(solution)/shard_map/reduce_scatter | solution.py:106
  256.1 122.6 %reduce-scatter.9.cloned.1.call-start = ((), (), s32[]{:S(2)}) async-start(), calls=%async_computation.7 | async-start | bytes 327680 | tf_op jit(solution)/shard_map/reduce_scatter | solution.py:105
  (8 other events, 88.6 us)
Sparse Core Ops, SparseCore 0:
  64.7 63.7 reduce-scatter.6
  130.9 19.0 reduce-scatter.4
  256.3 62.8 reduce-scatter.10
  321.4 19.1 reduce-scatter.8
Sparse Core Ops, SparseCore 1:
  74.2 125.7 all-reduce.2
  250.7 124.8 all-reduce.4
